TPU v7x, 32 devices: a whole 2x2x4 slice. The times are simulated.
32 devices in a mesh: groups: 1, rows: 16 (over z, y, core), heads: 2 (over x).
Axes of the slice: x: 2, y: 2, z: 4, core: 2. Of those that a mesh axis runs over, the one named last changes fastest.
Arguments:
- queries: bfloat16 [2048, 8192], P(('groups', 'rows'), 'heads'), may hold values from -40 to 40
- passages: bfloat16 [768, 1024], P(('groups', 'rows')), may hold values from -6 to 6
- enc_gain: bfloat16 [1024], replicated, may hold values from 0.099609375 to 1.8984375
- key_weight: bfloat16 [1024, 8192], P(None, 'heads'), may hold values from -0.1875 to 0.1875
- value_weight: bfloat16 [1024, 8192], P(None, 'heads'), may hold values from -0.1875 to 0.1875
- out_weight: bfloat16 [8192, 1024], P('heads'), may hold values from -0.125 to 0.125
- passage_length: int32 [3], P('groups'), may hold values from 64 to 256, as said below
Outputs:
- cross_out: bfloat16 [2048, 1024], P(('groups', 'rows'))
Inputs may be any that keep to these rules, and one draw needn't show every extreme that they name: `passage_length`: every passage has at least a quarter of its padded tokens; some passage is full and some has exactly 64 tokens.
All inputs are finite; a program needn't handle non-finite values.
Results may differ from a plain program's by a relative error of at most 0.012.
The roundings to bfloat16 on the way count: a program that leaves them out, or rounds other values in their place, can miss the bound.
Values may be sent and summed in bfloat16 or wider, within the bound.
A program may use at most 128 MiB of HBM per device.

v0:
```python
import jax
import jax.numpy as jnp
from jax import lax
from jax.sharding import PartitionSpec as P

DK = 128
PASS_LEN = 256


LOWEST = -1e30


def normalize(rows_in, enc_gain):
    wide = rows_in.astype(jnp.float32)
    mean_square = jnp.mean(wide * wide, axis=-1, keepdims=True)
    return (wide * lax.rsqrt(mean_square + 1e-06) * enc_gain.astype(jnp.float32)).astype(
        jnp.bfloat16
    )


def project(rows_in, enc_gain, key_weight, value_weight):
    normed = normalize(rows_in, enc_gain)
    key_rows = jnp.dot(normed, key_weight, preferred_element_type=jnp.float32).astype(jnp.bfloat16)
    value_rows = jnp.dot(normed, value_weight, preferred_element_type=jnp.float32).astype(
        jnp.bfloat16
    )
    return (key_rows, value_rows)


def row_mask(passage_length, number):
    positions = jnp.arange(number, dtype=jnp.int32)
    owner = positions // PASS_LEN
    offset = positions % PASS_LEN
    matches = owner[:, None] == jnp.arange(passage_length.shape[0], dtype=jnp.int32)[None, :]
    row_length = jnp.sum(jnp.where(matches, passage_length[None, :], 0), axis=1)
    return offset < row_length


def attend(carry, query_heads, key_rows, value_rows, passage_length):
    best, denom, summed = carry
    number = key_rows.shape[0]
    heads_here = query_heads.shape[1]
    key_heads = key_rows.reshape(number, heads_here, DK)
    value_heads = value_rows.reshape(number, heads_here, DK)
    scores = jnp.einsum("thd,ehd->hte", query_heads, key_heads, preferred_element_type=jnp.float32)
    valid = row_mask(passage_length, number)[None, None, :]
    masked = jnp.where(valid, scores, LOWEST)
    new_best = jnp.maximum(best, jnp.max(masked, axis=-1))
    expo = jnp.where(valid, jnp.exp(scores - new_best[:, :, None]), 0.0)
    factor = jnp.exp(best - new_best)
    denom = jnp.sum(expo, axis=-1)
    mixed = jnp.einsum(
        "hte,ehd->thd", expo.astype(jnp.bfloat16), value_heads, preferred_element_type=jnp.float32
    )
    summed = summed * factor.T[:, :, None] + mixed
    return (new_best, denom, summed)


def on_device(queries, passages, enc_gain, key_weight, value_weight, out_weight, passage_length):
    rows_here = queries.shape[0]
    inner = queries.shape[1]
    heads_here = inner // DK
    query_heads = queries.reshape(rows_here, heads_here, DK)
    start_carry = (
        jnp.full((heads_here, rows_here), LOWEST, jnp.float32),
        jnp.zeros((heads_here, rows_here), jnp.float32),
        jnp.zeros((rows_here, heads_here, DK), jnp.float32),
    )
    key_rows, value_rows = project(
        lax.all_gather(passages, "rows", axis=0, tiled=True), enc_gain, key_weight, value_weight
    )
    best, denom, summed = attend(start_carry, query_heads, key_rows, value_rows, passage_length)
    attended = (summed / denom.T[:, :, None]).astype(jnp.bfloat16).reshape(rows_here, inner)
    partial_out = jnp.dot(attended, out_weight, preferred_element_type=jnp.float32)
    share = lax.psum_scatter(
        partial_out.astype(jnp.bfloat16), "heads", scatter_dimension=1, tiled=True
    )
    cross_out = lax.all_gather(share, "heads", axis=1, tiled=True)
    return cross_out


def solution(mesh):
    return jax.shard_map(
        on_device,
        mesh=mesh,
        in_specs=(
            P(("groups", "rows"), "heads"),
            P(("groups", "rows"), None),
            P(),
            P(None, "heads"),
            P(None, "heads"),
            P("heads", None),
            P("groups"),
        ),
        out_specs=P(("groups", "rows"), None),
        check_vma=False,
    )
```

profile of v0, /device:TPU:0, one launch (start us, length us, event | category | flops | bytes accessed | tf_op | source)
XLA Modules:
  0.0 132.5 jit_solution(18445588045736639414)
XLA Ops:
  6.5 0.0 copy-start
  6.5 0.0 all-gather.2.cloned.1.call-start
  6.5 0.7 all-gather.2.cloned.1.call-update
  7.3 0.0 reduce-scatter.2.cloned.1.call-start
  7.3 0.7 convert_element_type.25
  8.0 0.7 select_reduce_fusion.1
  8.7 43.2 %all-gather.2.cloned.1.call-done = bf16[768,1024]{1,0:T(8,128)(2,1)} async-done(((bf16[48,1024]{1,0:T(8,128)(2,1)}), bf16[768,1024]{1,0:T(8,128)(2,1)}) %all-gather.2.cloned.1.call-update) | async-done | bytes 1572880 | tf_op jit(solution)/shard_map/all_gather | solution.py:70
  52.0 1.8 %fusion.7 = f32[768]{0:T(1024)S(1)} fusion(bf16[768,1024]{1,0:T(8,128)(2,1)} %all-gather.2.cloned.1.call-done), kind=kLoop, calls=%fused_computation.15 | loop fusion | flops 2358528 | bytes 1575936 | tf_op jit(solution)/shard_map/reduce_sum | solution.py:15
  53.8 12.5 %convolution_convert_fusion = bf16[768,4096]{1,0:T(8,128)(2,1)} fusion(bf16[1024,4096]{1,0:T(8,128)(2,1)} %param.11, bf16[768,1024]{1,0:T(8,128)(2,1)} %all-gather.2.cloned.1.call-done, f32[1024]{0:T(1024)S(1)} %convert_element_type.25, f32[768]{0:T(1024)S(1)} %add_rsqrt_fusion), kind=kOutput, calls=%fused_computation.4 | convolution fusion | flops 6448742400 | bytes 16260096 | tf_op jit(solution)/shard_map/dot_general | solution.py:24
  66.2 0.0 copy-start.2
  66.2 8.8 %copy.17 = bf16[768,4096]{0,1:T(8,128)(2,1)} copy(bf16[768,4096]{1,0:T(8,128)(2,1)} %convolution_convert_fusion) | data formatting | bytes 12582912 | tf_op jit(solution)/shard_map/reshape | solution.py:44
  75.1 0.0 copy-done.2
  75.1 12.2 %fusion.10 = bf16[96,32,8,128]{3,2,1,0:T(8,128)(2,1)} fusion(bf16[1024,4096]{1,0:T(8,128)(2,1)} %param.10, bf16[768,1024]{1,0:T(8,128)(2,1)S(1)} %copy-done.2, f32[1024]{0:T(1024)S(1)} %convert_element_type.25, f32[768]{0:T(1024)S(1)} %add_rsqrt_fusion), kind=kOutput, calls=%fused_computation.18 | convolution fusion | flops 6448742400 | bytes 16260096 | tf_op jit(solution)/shard_map/dot_general | solution.py:23
  87.2 0.0 copy-done
  87.2 4.2 %select_reduce_fusion = (f32[32,128]{1,0:T(8,128)S(1)}, f32[32,768,128]{2,1,0:T(8,128)S(1)}) fusion(pred[768]{0:T(1024)(128)(4,1)S(1)} %fusion.17, bf16[96,32,8,128]{3,2,1,0:T(8,128)(2,1)} %fusion.10, bf16[128,4096]{1,0:T(8,128)(2,1)S(1)} %copy-done), kind=kOutput, calls=%fused_computation.3 | convolution fusion | flops 811593728 | bytes 19940096 | tf_op jit(solution)/shard_map/thd,ehd->hte/dot_general | solution.py:45
  91.5 0.0 copy-start.1
  91.5 0.0 slice-start
  91.5 2.9 %bitcast_reduce_fusion = f32[32,128]{1,0:T(8,128)S(1)} fusion(f32[32,768,128]{2,1,0:T(8,128)S(1)} %get-tuple-element.8, f32[32,128]{1,0:T(8,128)S(1)} %get-tuple-element.6, pred[768]{0:T(1024)(128)(4,1)S(1)} %fusion.17), kind=kLoop, calls=%fused_computation | loop fusion | flops 9433088 | bytes 12616448 | tf_op jit(solution)/shard_map/reduce_sum | solution.py:51
  94.4 2.7 %copy-done.1 = f32[32,768,128]{2,1,0:T(8,128)} copy-done((f32[32,768,128]{2,1,0:T(8,128)}, f32[32,768,128]{2,1,0:T(8,128)S(1)}, u32[]{:S(2)}) %copy-start.1) | copy-done | bytes 12582936
  97.2 0.0 slice-start.1
  97.2 9.2 %fusion.12 = bf16[128,32,128]{0,2,1:T(8,128)(2,1)S(1)} fusion(bf16[768,32,128]{0,2,1:T(8,128)(2,1)} %bitcast.40, f32[32,768,128]{2,1,0:T(8,128)} %copy-done.1, f32[32,128]{1,0:T(8,128)S(1)} %get-tuple-element.6, pred[768]{0:T(1024)(128)(4,1)S(1)} %fusion.17, f32[128,32]{0,1:T(8,128)S(1)} %bitcast.42, f32[128,32]{0,1:T(8,128)S(1)} %get-tuple-element.5), kind=kOutput, calls=%fused_computation.21 | convolution fusion | flops 816316416 | bytes 19972864 | tf_op jit(solution)/shard_map/hte,ehd->thd/dot_general | solution.py:52
  106.4 0.0 slice-done
  106.4 0.0 slice-done.1
  106.4 2.0 %convolution_convert_fusion.2 = bf16[128,1024]{1,0:T(8,128)(2,1)} fusion(bf16[128,4096]{0,1:T(8,128)(2,1)S(1)} %bitcast.41, bf16[4096,1024]{1,0:T(8,128)(2,1)S(1)} %bitcast.39), kind=kOutput, calls=%fused_computation.22 | convolution fusion | flops 1073872896 | bytes 9699328 | tf_op jit(solution)/shard_map/dot_general | solution.py:74
  108.4 0.0 reduce-scatter.2.cloned.1.call-update
  108.4 10.6 %reduce-scatter.2.cloned.1.call-done = bf16[128,512]{1,0:T(8,128)(2,1)} async-done(((bf16[128,1024]{1,0:T(8,128)(2,1)}), bf16[128,512]{1,0:T(8,128)(2,1)}) %reduce-scatter.2.cloned.1.call-update) | async-done | bytes 131088 | tf_op jit(solution)/shard_map/reduce_scatter | solution.py:75
  119.0 5.9 %all_gather.7 = bf16[128,1024]{1,0:T(8,128)(2,1)S(1)} all-gather(bf16[128,512]{1,0:T(8,128)(2,1)} %reduce-scatter.2.cloned.1.call-done), channel_id=1, replica_groups=mesh['groups'=1,'rows'=16,'heads'=2] {'heads'}, dimensions={1}, use_global_device_ids=true | all-gather | bytes 393216 | tf_op jit(solution)/shard_map/all_gather | solution.py:78
  125.0 0.7 copy.33
  (5 shorter events, 0.0 us)
Async XLA Ops:
  6.5 80.7 %copy-start = (bf16[128,4096]{1,0:T(8,128)(2,1)S(1)}, bf16[128,4096]{1,0:T(8,128)(2,1)}, u32[]{:S(2)}) copy-start(bf16[128,4096]{1,0:T(8,128)(2,1)} %param.7) | copy-start | bytes 3145732
  6.5 45.4 %all-gather.2.cloned.1.call-start = ((), (), s32[]{:S(2)}) async-start(), calls=%async_computation.1 | async-start | bytes 1671168 | tf_op jit(solution)/shard_map/all_gather | solution.py:70
  7.3 111.8 %reduce-scatter.2.cloned.1.call-start = ((), (), s32[]{:S(2)}) async-start(), calls=%async_computation.2 | async-start | bytes 393216 | tf_op jit(solution)/shard_map/reduce_scatter | solution.py:75
  66.2 8.8 %copy-start.2 = (bf16[768,1024]{1,0:T(8,128)(2,1)S(1)}, bf16[768,1024]{1,0:T(8,128)(2,1)}, u32[]{:S(2)}) copy-start(bf16[768,1024]{1,0:T(8,128)(2,1)} %all-gather.2.cloned.1.call-done) | copy-start | bytes 4718596
  91.5 5.7 %copy-start.1 = (f32[32,768,128]{2,1,0:T(8,128)}, f32[32,768,128]{2,1,0:T(8,128)S(1)}, u32[]{:S(2)}) copy-start(f32[32,768,128]{2,1,0:T(8,128)S(1)} %get-tuple-element.8) | copy-start | bytes 37748740
  91.5 14.9 %slice-start = ((s8[8388608]{0:T(1024)(128)(4,1)}), s8[4194304]{0:T(1024)(128)(4,1)S(1)}, s32[]{:S(2)}) async-start(s8[8388608]{0:T(1024)(128)(4,1)} %bitcast.38), calls=%async_computation.3 | async-start | bytes 8388608
  97.2 9.2 %slice-start.1 = ((s8[8388608]{0:T(1024)(128)(4,1)}), s8[4194304]{0:T(1024)(128)(4,1)S(1)}, s32[]{:S(2)}) async-start(s8[8388608]{0:T(1024)(128)(4,1)} %bitcast.38), calls=%async_computation.4 | async-start | bytes 8388608
Sparse Core Ops, SparseCore 0:
  9.6 42.3 all-gather.1
  108.5 10.4 reduce-scatter.1
where the time goes:
time: 133 us
  waiting for transfers between devices  54.6 us (41%)
  matrix products  40 us (30%)
  between operations  13.5 us (10%)
  local copies, waits for them, and re-layouts  12.3 us (9%)
  other arithmetic  6.14 us (5%)
  blocking collectives  5.95 us (4%)
    all_gather x1, waiting for transfers between devices, on_device(): lax.all_gather(passages, 'rows', axis=0, tiled=True)  43.2 us
    dot_general x1, matrix products, project(): jnp.dot(normed, value_weight, preferred_element_type=jnp.float32)  12.5 us
    dot_general x1, matrix products, project(): jnp.dot(normed, key_weight, preferred_element_type=jnp.float32)  12.2 us
    reduce_scatter x1, waiting for transfers between devices, on_device(): lax.psum_scatter(partial_out.astype(jnp.bfloat16), 'heads', scatter_dimen...  10.6 us
    dot_general x1, matrix products, attend(): jnp.einsum('hte,ehd->thd', expo.astype(jnp.bfloat16), value_heads, prefer...  9.19 us
    reshape x1, local copies, waits for them, and re-layouts, attend(): value_heads = value_rows.reshape(number, heads_here, DK)  8.82 us
    all_gather x1, blocking collectives, on_device(): cross_out = lax.all_gather(share, 'heads', axis=1, tiled=True)  5.95 us
    dot_general x1, matrix products, attend(): jnp.einsum('thd,ehd->hte', query_heads, key_heads, preferred_element_type...  4.22 us
  transfers between devices with their start and end apart: 2, of which 2 were waited for; matrix products, arithmetic and copies ran while one was open for 1% of the time, Pallas kernels for 0%

commit v1 on v0

v1 whole, which is shorter than its diff:
```python
import functools

import jax
import jax.numpy as jnp
from jax import lax
from jax.experimental import pallas as pl
from jax.experimental.pallas import tpu as pltpu
from jax.sharding import PartitionSpec as P

DK = 128
PASS_LEN = 256
SHORT_LEN = PASS_LEN // 4
LOWEST = -1e30
MESH = pl.DeviceIdType.MESH
LOADS = 4
GROUP = 2 * DK
OUT_CHUNK = 256


def flip(index, bits):
    bit = 1
    while bit <= bits:
        if bits & bit:
            index = index + bit - 2 * bit * ((index // bit) % 2)
        bit *= 2
    return index


def kernel(
    n_rows,
    n_heads,
    length_ref,
    queries_ref,
    passages_ref,
    gain_ref,
    key_ref,
    value_ref,
    outw_ref,
    out_ref,
    rows_all,
    normed,
    query_buf,
    key_w,
    value_w,
    out_w,
    keys,
    values,
    attended,
    core_send,
    core_recv,
    x_parts,
    local_sem,
    load_sem,
    z_send_sem,
    y_send_sem,
    x_send_sem,
    core_send_sem,
    main_recv,
    rest_recv,
    query_sem,
    out_core_sem,
    out_x_sem,
):
    block, width = passages_ref.shape
    dec, inner = queries_ref.shape
    half = inner // 2
    n_pass = length_ref.shape[0]
    n_z = n_rows // 4
    wide = width * 5 // 8
    narrow = width - wide

    me = lax.axis_index("rows")
    x = lax.axis_index("heads")
    core = me % 2
    y = (me // 2) % 2
    z = me // 4

    def row_of(z_, y_, c_):
        return (z_ * 2 + y_) * 2 + c_

    def at_row(r):
        return {"rows": r}

    partner = at_row(flip(me, 1))
    across_y = at_row(flip(me, 2))
    side = x % 2
    x_peers = [{"heads": flip(x, d)} for d in range(1, n_heads)]
    across_x = x_peers[0]

    def rows_at(r):
        return pl.ds(pl.multiple_of(r * block, 16), block)

    main_cols = pl.ds(pl.multiple_of(side * narrow, 128), wide)
    rest_cols = pl.ds(pl.multiple_of((1 - side) * wide, 128), narrow)
    give_cols = pl.ds(pl.multiple_of(side * wide, 128), narrow)

    own_rows = pltpu.make_async_copy(passages_ref, rows_all.at[rows_at(me)], local_sem.at[0])
    own_rows.start()
    mine = pl.ds(pl.multiple_of(core * half, 128), half)
    theirs = pl.ds(pl.multiple_of((1 - core) * half, 128), half)
    my_t = pl.ds(pl.multiple_of(core * dec, 128), dec)
    own_queries = pltpu.make_async_copy(
        queries_ref.at[:, mine], query_buf.at[my_t], local_sem.at[1]
    )
    own_queries.start()
    loads = []
    share = half // LOADS
    for part in range(LOADS):
        here = pl.ds(part * share, share)
        there = pl.ds(pl.multiple_of(core * half + part * share, 128), share)
        loads.append(
            (
                pltpu.make_async_copy(
                    key_ref.at[:, there], key_w.at[:, here], load_sem.at[0, part]
                ),
                pltpu.make_async_copy(
                    value_ref.at[:, there], value_w.at[:, here], load_sem.at[1, part]
                ),
                pltpu.make_async_copy(outw_ref.at[there], out_w.at[here], load_sem.at[2, part]),
            )
        )

    barrier = pltpu.get_barrier_semaphore()
    z_peers = [row_of(flip(z, d), y, core) for d in range(1, n_z)]
    peers = [at_row(r) for r in z_peers] + [across_y, partner] + x_peers
    for peer in peers:
        pl.semaphore_signal(barrier, inc=1, device_id=peer, device_id_type=MESH)
    pl.semaphore_wait(barrier, len(peers))

    sent = []

    def send(src, dst, send_sem, recv_sem, to):
        copy = pltpu.make_async_remote_copy(
            src_ref=src, dst_ref=dst, send_sem=send_sem, recv_sem=recv_sem,
            device_id=to, device_id_type=MESH,
        )
        copy.start()
        sent.append(copy)

    def send_block(r, cols, send_sem, recv_sem, to):
        view = rows_all.at[rows_at(r), cols]
        send(view, view, send_sem, recv_sem.at[r], to)

    def await_block(r, cols, recv_sem):
        view = rows_all.at[rows_at(r), cols]
        pltpu.make_async_copy(view, view, recv_sem.at[r]).wait()

    own_rows.wait()
    for d in range(1, n_z):
        send_block(me, main_cols, z_send_sem.at[d - 1], main_recv, at_row(z_peers[d - 1]))
    send_block(me, main_cols, y_send_sem.at[0], main_recv, across_y)
    send_block(me, main_cols, core_send_sem.at[0, 0], main_recv, partner)
    send_block(me, rest_cols, core_send_sem.at[1, 0], rest_recv, partner)
    send(
        queries_ref.at[:, theirs], query_buf.at[my_t], query_sem.at[0], query_sem.at[1], partner
    )
    for triple in loads:
        triple[0].start()
        triple[1].start()
    for triple in loads:
        triple[2].start()

    others = []
    from_y = row_of(z, 1 - y, core)
    order = [("y", from_y, 0)]
    for d in range(1, n_z):
        order.append(("z", z_peers[d - 1], d))
        order.append(("y", row_of(flip(z, d), 1 - y, core), d))
    for number, (kind, r, d) in enumerate(order):
        await_block(r, main_cols, main_recv)
        if kind == "z":
            send_block(r, main_cols, y_send_sem.at[d], main_recv, across_y)
        send_block(r, give_cols, x_send_sem.at[number], rest_recv, across_x)
        send_block(r, main_cols, core_send_sem.at[0, number + 1], main_recv, partner)
        others.append(r)
    for number, r in enumerate(others):
        await_block(r, rest_cols, rest_recv)
        send_block(r, rest_cols, core_send_sem.at[1, number + 1], rest_recv, partner)
    for r in [me] + others:
        await_block(flip(r, 1), main_cols, main_recv)
        await_block(flip(r, 1), rest_cols, rest_recv)

    lengths = [length_ref[p] for p in range(n_pass)]
    is_short = []
    open_still = jnp.int32(1)
    for p in range(n_pass):
        hit = open_still * (lengths[p] == SHORT_LEN).astype(jnp.int32)
        is_short.append(hit)
        open_still = open_still - hit
    passed = []
    seen = jnp.int32(0)
    for p in range(n_pass):
        seen = seen + is_short[p]
        passed.append(seen)
    gain = gain_ref[...].astype(jnp.float32)
    sizes = [PASS_LEN] * (n_pass - 1) + [SHORT_LEN]
    number = sum(sizes)
    offsets = lax.broadcasted_iota(jnp.int32, (1, number), 1)
    bias = jnp.zeros((1, number), jnp.float32)

    def lanes(flag, shape):
        return jnp.full(shape, flag, jnp.int32) == 1

    def normalize(start, raw):
        wide_rows = raw.astype(jnp.float32)
        mean_square = jnp.mean(wide_rows * wide_rows, axis=-1, keepdims=True)
        normed[start : start + raw.shape[0], :] = (
            wide_rows * lax.rsqrt(mean_square + 1e-06) * gain
        ).astype(jnp.bfloat16)

    step = SHORT_LEN
    for p in range(n_pass - 1):
        length = lengths[p] + passed[p] * (lengths[p + 1] - lengths[p])
        bad = (offsets >= p * PASS_LEN + length) & (offsets < (p + 1) * PASS_LEN)
        bias = jnp.where(bad, LOWEST, bias)
        moved = lanes(passed[p], (step, width))
        for row in range(p * PASS_LEN, (p + 1) * PASS_LEN, step):
            here = rows_all[row : row + step, :].astype(jnp.float32)
            after = rows_all[row + PASS_LEN : row + PASS_LEN + step, :].astype(jnp.float32)
            normalize(row, jnp.where(moved, after, here))
    last = rows_all[0:step, :].astype(jnp.float32)
    for p in range(1, n_pass):
        place = p * PASS_LEN
        here = rows_all[place : place + step, :].astype(jnp.float32)
        last = jnp.where(lanes(is_short[p], (step, width)), here, last)
    normalize((n_pass - 1) * PASS_LEN, last)

    for triple in loads:
        triple[0].wait()
        triple[1].wait()
    own_queries.wait()
    other_t = pl.ds(pl.multiple_of((1 - core) * dec, 128), dec)
    pltpu.make_async_copy(query_buf.at[other_t], query_buf.at[other_t], query_sem.at[1]).wait()

    groups = half // GROUP

    def project(g):
        cols = slice(g * GROUP, (g + 1) * GROUP)
        keys[g % 2] = jnp.dot(
            normed[...], key_w[:, cols], preferred_element_type=jnp.float32
        ).astype(jnp.bfloat16)
        values[g % 2] = jnp.dot(
            normed[...], value_w[:, cols], preferred_element_type=jnp.float32
        ).astype(jnp.bfloat16)

    def attend(g):
        for h in range(GROUP // DK):
            inside = slice(h * DK, (h + 1) * DK)
            cols = slice(g * GROUP + h * DK, g * GROUP + (h + 1) * DK)
            scores = lax.dot_general(
                query_buf[:, cols],
                keys[g % 2, :, inside],
                (((1,), (1,)), ((), ())),
                preferred_element_type=jnp.float32,
            )
            scores = scores + bias
            top = jnp.max(scores, axis=-1, keepdims=True)
            expo = jnp.exp(scores - top)
            denom = jnp.sum(expo, axis=-1, keepdims=True)
            mixed = jnp.dot(
                expo.astype(jnp.bfloat16),
                values[g % 2, :, inside],
                preferred_element_type=jnp.float32,
            )
            attended[:, cols] = (mixed / denom).astype(jnp.bfloat16)

    project(0)
    for g in range(groups):
        if g + 1 < groups:
            project(g + 1)
        attend(g)

    for triple in loads:
        triple[2].wait()
    chunks = width // OUT_CHUNK

    def chunk_of(j):
        return slice(j * OUT_CHUNK, (j + 1) * OUT_CHUNK)

    mine_parts = []
    for j in range(chunks):
        cols = chunk_of(j)
        core_send[:, cols] = jnp.dot(
            attended[other_t, :], out_w[:, cols], preferred_element_type=jnp.float32
        ).astype(jnp.bfloat16)
        send(
            core_send.at[:, cols], core_recv.at[:, cols], out_core_sem.at[0, j],
            out_core_sem.at[1, j], partner,
        )
        mine_parts.append(
            jnp.dot(attended[my_t, :], out_w[:, cols], preferred_element_type=jnp.float32)
        )
    for j in range(chunks):
        cols = chunk_of(j)
        view = core_recv.at[:, cols]
        pltpu.make_async_copy(view, view, out_core_sem.at[1, j]).wait()
        x_parts[x, :, cols] = (mine_parts[j] + core_recv[:, cols].astype(jnp.float32)).astype(
            jnp.bfloat16
        )
        view = x_parts.at[x, :, cols]
        for d, peer in enumerate(x_peers):
            send(view, view, out_x_sem.at[0, d, j], out_x_sem.at[1, d, j], peer)
    for j in range(chunks):
        cols = chunk_of(j)
        for d in range(1, n_heads):
            view = x_parts.at[flip(x, d), :, cols]
            pltpu.make_async_copy(view, view, out_x_sem.at[1, d - 1, j]).wait()
        total = x_parts[0, :, cols].astype(jnp.float32)
        for term in range(1, n_heads):
            total += x_parts[term, :, cols].astype(jnp.float32)
        out_ref[:, cols] = total.astype(jnp.bfloat16)
    for copy in sent:
        copy.wait_send()


def on_device(
    n_rows, n_heads, queries, passages, enc_gain, key_weight, value_weight, out_weight, passage_length
):
    dec, inner = queries.shape
    block, width = passages.shape
    half = inner // 2
    n_pass = passage_length.shape[0]
    number = (n_pass - 1) * PASS_LEN + SHORT_LEN
    n_z = n_rows // 4
    same = n_rows // 2
    chunks = width // OUT_CHUNK
    bf16 = jnp.bfloat16
    dma = pltpu.SemaphoreType.DMA
    vmem = pl.BlockSpec(memory_space=pltpu.VMEM)
    anywhere = pl.BlockSpec(memory_space=pl.ANY)
    return pl.pallas_call(
        functools.partial(kernel, n_rows, n_heads),
        out_shape=jax.ShapeDtypeStruct((dec, width), bf16),
        in_specs=[
            pl.BlockSpec(memory_space=pltpu.SMEM),
            anywhere,
            anywhere,
            vmem,
            anywhere,
            anywhere,
            anywhere,
        ],
        out_specs=vmem,
        scratch_shapes=[
            pltpu.VMEM((n_rows * block, width), bf16),
            pltpu.VMEM((number, width), bf16),
            pltpu.VMEM((2 * dec, half), bf16),
            pltpu.VMEM((width, half), bf16),
            pltpu.VMEM((width, half), bf16),
            pltpu.VMEM((half, width), bf16),
            pltpu.VMEM((2, number, GROUP), bf16),
            pltpu.VMEM((2, number, GROUP), bf16),
            pltpu.VMEM((2 * dec, half), bf16),
            pltpu.VMEM((dec, width), bf16),
            pltpu.VMEM((dec, width), bf16),
            pltpu.VMEM((n_heads, dec, width), bf16),
            dma((2,)),
            dma((3, LOADS)),
            dma((n_z - 1,)),
            dma((n_z,)),
            dma((same,)),
            dma((2, same)),
            dma((n_rows,)),
            dma((n_rows,)),
            dma((2,)),
            dma((2, chunks)),
            dma((2, n_heads - 1, chunks)),
        ],
        compiler_params=pltpu.CompilerParams(
            collective_id=0, has_side_effects=True, vmem_limit_bytes=60 * 1024 * 1024
        ),
    )(
        passage_length,
        queries,
        passages,
        enc_gain.reshape(1, width),
        key_weight,
        value_weight,
        out_weight,
    )


def solution(mesh):
    return jax.shard_map(
        functools.partial(on_device, mesh.shape["rows"], mesh.shape["heads"]),
        mesh=mesh,
        in_specs=(
            P(("groups", "rows"), "heads"),
            P(("groups", "rows"), None),
            P(),
            P(None, "heads"),
            P(None, "heads"),
            P("heads", None),
            P("groups"),
        ),
        out_specs=P(("groups", "rows"), None),
        check_vma=False,
    )
```

time: 133 us -> 50.5 us (0.38)
  waiting for transfers between devices: 54.6 us -> 0 us
  Pallas kernels: 0 us -> 47.3 us
  matrix products: 40 us -> 0 us
  between operations: 13.5 us -> 0.01 us
  local copies, waits for them, and re-layouts: 12.3 us -> 2.95 us
  other arithmetic: 6.14 us -> 0 us
  blocking collectives: 5.95 us -> 0 us
    pallas_call x0 -> x1, Pallas kernels: none -> 47.3 us  [on_device(): pl.pallas_call(functools.partial(kernel, n_rows, n_heads), out_shape=jax....]
    all_gather x1 -> x0, waiting for transfers between devices: 43.2 us -> none  [on_device(): lax.all_gather(passages, 'rows', axis=0, tiled=True)]
    dot_general x5 -> x0, matrix products: 40 us -> none  [the longest x1 12.5 us: project(): jnp.dot(normed, value_weight, preferred_element_type=jnp.float32)]
    reduce_scatter x1 -> x0, waiting for transfers between devices: 10.6 us -> none  [on_device(): lax.psum_scatter(partial_out.astype(jnp.bfloat16), 'heads', scatter_dimen...]
    reshape x1, local copies, waits for them, and re-layouts: 8.82 us -> 1.28 us  [on_device(): enc_gain.reshape(1, width)]
    all_gather x1 -> x0, blocking collectives: 5.95 us -> none  [on_device(): cross_out = lax.all_gather(share, 'heads', axis=1, tiled=True)]
    reduce_sum x3 -> x0, other arithmetic: 5.43 us -> none  [the longest x1 2.91 us: attend(): denom = jnp.sum(expo, axis=-1)]
    unnamed x11 -> x1, local copies, waits for them, and re-layouts: 3.47 us -> 1.67 us
  transfers between devices with their start and end apart: 2 -> 0, of which waited for: 2 -> 0; matrix products, arithmetic and copies ran while one was open for 1% -> 0% of each run, Pallas kernels for 0% -> 0%
where the time goes in v1:
time: 50.5 us; the launch traced here: 50.3 us
  Pallas kernels  47.3 us (94%)
  local copies, waits for them, and re-layouts  2.95 us (6%)
    pallas_call x1, Pallas kernels, on_device(): pl.pallas_call(functools.partial(kernel, n_rows, n_heads), out_shape=jax....  47.3 us
    unnamed x1, local copies, waits for them, and re-layouts  1.67 us
    reshape x1, local copies, waits for them, and re-layouts, on_device(): enc_gain.reshape(1, width)  1.28 us

profile of v1, /device:TPU:0, one launch (start us, length us, event | category | flops | bytes accessed | tf_op | source)
XLA Modules:
  0.0 50.3 jit_solution(17741706390634928)
XLA Ops:
  0.0 1.3 %reshape.3.gain_ref = bf16[1,1024]{1,0:T(2,128)(2,1)} reshape(bf16[1024]{0:T(1024)(128)(2,1)} %param.9) | data formatting | bytes 4096 | tf_op jit(solution)/shard_map/reshape | solution.py:376
  1.3 47.3 %shard_map.73 = bf16[128,1024]{1,0:T(8,128)(2,1)} custom-call(s32[3]{0:T(128)} %length_ref.1, bf16[128,4096]{1,0:T(8,128)(2,1)} %queries_ref.1, bf16[48,1024]{1,0:T(8,128)(2,1)} %passages_ref.1, bf16[1,1024]{1,0:T(2,128)(2,1)} %reshape.3.gain_ref, bf16[1024,4096]{1,0:T(8,128)(2,1)} %key_ref.1, bf16[1024,4096]{1,0:T(8,128)(2,1)} %value_ref.1, ...), custom_call_target="tpu_custom_call" | custom-call | tf_op jit(solution)/shard_map/pallas_call | solution.py:331
  48.6 1.7 %copy.9 = bf16[128,1024]{1,0:T(8,128)(2,1)} copy(bf16[128,1024]{1,0:T(8,128)(2,1)} %shard_map.73) | data formatting | bytes 524288

commit v2 on v1

--- a/solution.py
+++ b/solution.py
@@ -38,6 +38,7 @@
     outw_ref,
     out_ref,
     rows_all,
+    norm_all,
     normed,
     query_buf,
     key_w,
@@ -48,6 +49,7 @@
     attended,
     core_send,
     core_recv,
+    own_part,
     x_parts,
     local_sem,
     load_sem,
@@ -145,12 +147,16 @@
         view = rows_all.at[rows_at(r), cols]
         pltpu.make_async_copy(view, view, recv_sem.at[r]).wait()
 
-    own_rows.wait()
+    def send_own(cols, send_sem, recv_sem, to):
+        send(
+            passages_ref.at[:, cols], rows_all.at[rows_at(me), cols], send_sem, recv_sem.at[me], to
+        )
+
     for d in range(1, n_z):
-        send_block(me, main_cols, z_send_sem.at[d - 1], main_recv, at_row(z_peers[d - 1]))
-    send_block(me, main_cols, y_send_sem.at[0], main_recv, across_y)
-    send_block(me, main_cols, core_send_sem.at[0, 0], main_recv, partner)
-    send_block(me, rest_cols, core_send_sem.at[1, 0], rest_recv, partner)
+        send_own(main_cols, z_send_sem.at[d - 1], main_recv, at_row(z_peers[d - 1]))
+    send_own(main_cols, y_send_sem.at[0], main_recv, across_y)
+    send_own(main_cols, core_send_sem.at[0, 0], main_recv, partner)
+    send_own(rest_cols, core_send_sem.at[1, 0], rest_recv, partner)
     send(
         queries_ref.at[:, theirs], query_buf.at[my_t], query_sem.at[0], query_sem.at[1], partner
     )
@@ -165,7 +171,9 @@
     order = [("y", from_y, 0)]
     for d in range(1, n_z):
         order.append(("z", z_peers[d - 1], d))
-        order.append(("y", row_of(flip(z, d), 1 - y, core), d))
+        if d > 1:
+            order.append(("y", row_of(flip(z, d - 1), 1 - y, core), d - 1))
+    order.append(("y", row_of(flip(z, n_z - 1), 1 - y, core), n_z - 1))
     for number, (kind, r, d) in enumerate(order):
         await_block(r, main_cols, main_recv)
         if kind == "z":
@@ -173,12 +181,30 @@
         send_block(r, give_cols, x_send_sem.at[number], rest_recv, across_x)
         send_block(r, main_cols, core_send_sem.at[0, number + 1], main_recv, partner)
         others.append(r)
+    gain = gain_ref[...].astype(jnp.float32).reshape(1, width)
+
+    def normalize(r):
+        wide_rows = rows_all[rows_at(r), :].astype(jnp.float32)
+        mean_square = jnp.mean(wide_rows * wide_rows, axis=-1, keepdims=True)
+        norm_all[rows_at(r), :] = (
+            wide_rows * lax.rsqrt(mean_square + 1e-06) * gain
+        ).astype(jnp.bfloat16)
+
+    def normalize_partner(r):
+        await_block(flip(r, 1), main_cols, main_recv)
+        await_block(flip(r, 1), rest_cols, rest_recv)
+        normalize(flip(r, 1))
+
+    own_rows.wait()
+    normalize(me)
+    normalize_partner(me)
     for number, r in enumerate(others):
         await_block(r, rest_cols, rest_recv)
         send_block(r, rest_cols, core_send_sem.at[1, number + 1], rest_recv, partner)
-    for r in [me] + others:
-        await_block(flip(r, 1), main_cols, main_recv)
-        await_block(flip(r, 1), rest_cols, rest_recv)
+        normalize(r)
+        if number:
+            normalize_partner(others[number - 1])
+    normalize_partner(others[-1])
 
     lengths = [length_ref[p] for p in range(n_pass)]
     is_short = []
@@ -192,7 +218,6 @@
     for p in range(n_pass):
         seen = seen + is_short[p]
         passed.append(seen)
-    gain = gain_ref[...].astype(jnp.float32)
     sizes = [PASS_LEN] * (n_pass - 1) + [SHORT_LEN]
     number = sum(sizes)
     offsets = lax.broadcasted_iota(jnp.int32, (1, number), 1)
@@ -200,13 +225,6 @@
 
     def lanes(flag, shape):
         return jnp.full(shape, flag, jnp.int32) == 1
-
-    def normalize(start, raw):
-        wide_rows = raw.astype(jnp.float32)
-        mean_square = jnp.mean(wide_rows * wide_rows, axis=-1, keepdims=True)
-        normed[start : start + raw.shape[0], :] = (
-            wide_rows * lax.rsqrt(mean_square + 1e-06) * gain
-        ).astype(jnp.bfloat16)
 
     step = SHORT_LEN
     for p in range(n_pass - 1):
@@ -215,15 +233,15 @@
         bias = jnp.where(bad, LOWEST, bias)
         moved = lanes(passed[p], (step, width))
         for row in range(p * PASS_LEN, (p + 1) * PASS_LEN, step):
-            here = rows_all[row : row + step, :].astype(jnp.float32)
-            after = rows_all[row + PASS_LEN : row + PASS_LEN + step, :].astype(jnp.float32)
-            normalize(row, jnp.where(moved, after, here))
-    last = rows_all[0:step, :].astype(jnp.float32)
+            here = norm_all[row : row + step, :].astype(jnp.float32)
+            after = norm_all[row + PASS_LEN : row + PASS_LEN + step, :].astype(jnp.float32)
+            normed[row : row + step, :] = jnp.where(moved, after, here).astype(jnp.bfloat16)
+    last = norm_all[0:step, :].astype(jnp.float32)
     for p in range(1, n_pass):
         place = p * PASS_LEN
-        here = rows_all[place : place + step, :].astype(jnp.float32)
+        here = norm_all[place : place + step, :].astype(jnp.float32)
         last = jnp.where(lanes(is_short[p], (step, width)), here, last)
-    normalize((n_pass - 1) * PASS_LEN, last)
+    normed[number - step : number, :] = last.astype(jnp.bfloat16)
 
     for triple in loads:
         triple[0].wait()
@@ -236,20 +254,23 @@
 
     def project(g):
         cols = slice(g * GROUP, (g + 1) * GROUP)
-        keys[g % 2] = jnp.dot(
+        keys[:, cols] = jnp.dot(
             normed[...], key_w[:, cols], preferred_element_type=jnp.float32
         ).astype(jnp.bfloat16)
-        values[g % 2] = jnp.dot(
+        values[:, cols] = jnp.dot(
             normed[...], value_w[:, cols], preferred_element_type=jnp.float32
         ).astype(jnp.bfloat16)
 
-    def attend(g):
+    def attend(g, low, high):
+        size = high - low
         for h in range(GROUP // DK):
-            inside = slice(h * DK, (h + 1) * DK)
             cols = slice(g * GROUP + h * DK, g * GROUP + (h + 1) * DK)
+            asked = jnp.concatenate(
+                [query_buf[low:high, cols], query_buf[dec + low : dec + high, cols]], axis=0
+            )
             scores = lax.dot_general(
-                query_buf[:, cols],
-                keys[g % 2, :, inside],
+                asked,
+                keys[:, cols],
                 (((1,), (1,)), ((), ())),
                 preferred_element_type=jnp.float32,
             )
@@ -259,56 +280,77 @@
             denom = jnp.sum(expo, axis=-1, keepdims=True)
             mixed = jnp.dot(
                 expo.astype(jnp.bfloat16),
-                values[g % 2, :, inside],
+                values[:, cols],
                 preferred_element_type=jnp.float32,
             )
-            attended[:, cols] = (mixed / denom).astype(jnp.bfloat16)
+            mixed = (mixed / denom).astype(jnp.bfloat16)
+            attended[low:high, cols] = mixed[:size]
+            attended[dec + low : dec + high, cols] = mixed[size:]
+
+    chunks = width // OUT_CHUNK
+
+    def chunk_of(j):
+        return slice(j * OUT_CHUNK, (j + 1) * OUT_CHUNK)
+
+    def core_rows(c, low, high):
+        return pl.ds(pl.multiple_of(c * dec + low, 16), high - low)
+
+    def to_core(n, low, high):
+        rows = slice(low, high)
+        for j in range(chunks):
+            cols = chunk_of(j)
+            core_send[rows, cols] = jnp.dot(
+                attended[core_rows(1 - core, low, high), :],
+                out_w[:, cols],
+                preferred_element_type=jnp.float32,
+            ).astype(jnp.bfloat16)
+            send(
+                core_send.at[rows, cols], core_recv.at[rows, cols], out_core_sem.at[0, n, j],
+                out_core_sem.at[1, n, j], partner,
+            )
+        for j in range(chunks):
+            cols = chunk_of(j)
+            own_part[rows, cols] = jnp.dot(
+                attended[core_rows(core, low, high), :],
+                out_w[:, cols],
+                preferred_element_type=jnp.float32,
+            )
+
+    def to_x(n, low, high):
+        rows = slice(low, high)
+        for j in range(chunks):
+            cols = chunk_of(j)
+            view = core_recv.at[rows, cols]
+            pltpu.make_async_copy(view, view, out_core_sem.at[1, n, j]).wait()
+            x_parts[x, rows, cols] = (
+                own_part[rows, cols] + core_recv[rows, cols].astype(jnp.float32)
+            ).astype(jnp.bfloat16)
+            view = x_parts.at[x, rows, cols]
+            for d, peer in enumerate(x_peers):
+                send(view, view, out_x_sem.at[0, n, d, j], out_x_sem.at[1, n, d, j], peer)
+
+    def finish(n, low, high):
+        rows = slice(low, high)
+        for j in range(chunks):
+            cols = chunk_of(j)
+            for d in range(1, n_heads):
+                view = x_parts.at[flip(x, d), rows, cols]
+                pltpu.make_async_copy(view, view, out_x_sem.at[1, n, d - 1, j]).wait()
+            total = x_parts[0, rows, cols].astype(jnp.float32)
+            for term in range(1, n_heads):
+                total += x_parts[term, rows, cols].astype(jnp.float32)
+            out_ref[rows, cols] = total.astype(jnp.bfloat16)
 
     project(0)
     for g in range(groups):
         if g + 1 < groups:
             project(g + 1)
-        attend(g)
-
+        attend(g, 0, dec)
     for triple in loads:
         triple[2].wait()
-    chunks = width // OUT_CHUNK
-
-    def chunk_of(j):
-        return slice(j * OUT_CHUNK, (j + 1) * OUT_CHUNK)
-
-    mine_parts = []
-    for j in range(chunks):
-        cols = chunk_of(j)
-        core_send[:, cols] = jnp.dot(
-            attended[other_t, :], out_w[:, cols], preferred_element_type=jnp.float32
-        ).astype(jnp.bfloat16)
-        send(
-            core_send.at[:, cols], core_recv.at[:, cols], out_core_sem.at[0, j],
-            out_core_sem.at[1, j], partner,
-        )
-        mine_parts.append(
-            jnp.dot(attended[my_t, :], out_w[:, cols], preferred_element_type=jnp.float32)
-        )
-    for j in range(chunks):
-        cols = chunk_of(j)
-        view = core_recv.at[:, cols]
-        pltpu.make_async_copy(view, view, out_core_sem.at[1, j]).wait()
-        x_parts[x, :, cols] = (mine_parts[j] + core_recv[:, cols].astype(jnp.float32)).astype(
-            jnp.bfloat16
-        )
-        view = x_parts.at[x, :, cols]
-        for d, peer in enumerate(x_peers):
-            send(view, view, out_x_sem.at[0, d, j], out_x_sem.at[1, d, j], peer)
-    for j in range(chunks):
-        cols = chunk_of(j)
-        for d in range(1, n_heads):
-            view = x_parts.at[flip(x, d), :, cols]
-            pltpu.make_async_copy(view, view, out_x_sem.at[1, d - 1, j]).wait()
-        total = x_parts[0, :, cols].astype(jnp.float32)
-        for term in range(1, n_heads):
-            total += x_parts[term, :, cols].astype(jnp.float32)
-        out_ref[:, cols] = total.astype(jnp.bfloat16)
+    to_core(0, 0, dec)
+    to_x(0, 0, dec)
+    finish(0, 0, dec)
     for copy in sent:
         copy.wait_send()
 
@@ -343,16 +385,18 @@
         out_specs=vmem,
         scratch_shapes=[
             pltpu.VMEM((n_rows * block, width), bf16),
+            pltpu.VMEM((n_rows * block, width), bf16),
             pltpu.VMEM((number, width), bf16),
             pltpu.VMEM((2 * dec, half), bf16),
             pltpu.VMEM((width, half), bf16),
             pltpu.VMEM((width, half), bf16),
             pltpu.VMEM((half, width), bf16),
-            pltpu.VMEM((2, number, GROUP), bf16),
-            pltpu.VMEM((2, number, GROUP), bf16),
+            pltpu.VMEM((number, half), bf16),
+            pltpu.VMEM((number, half), bf16),
             pltpu.VMEM((2 * dec, half), bf16),
             pltpu.VMEM((dec, width), bf16),
             pltpu.VMEM((dec, width), bf16),
+            pltpu.VMEM((dec, width), jnp.float32),
             pltpu.VMEM((n_heads, dec, width), bf16),
             dma((2,)),
             dma((3, LOADS)),
@@ -363,8 +407,8 @@
             dma((n_rows,)),
             dma((n_rows,)),
             dma((2,)),
-            dma((2, chunks)),
-            dma((2, n_heads - 1, chunks)),
+            dma((2, 1, chunks)),
+            dma((2, 1, n_heads - 1, chunks)),
         ],
         compiler_params=pltpu.CompilerParams(
             collective_id=0, has_side_effects=True, vmem_limit_bytes=60 * 1024 * 1024
@@ -373,7 +417,7 @@
         passage_length,
         queries,
         passages,
-        enc_gain.reshape(1, width),
+        enc_gain,
         key_weight,
         value_weight,
         out_weight,

time: 50.5 us -> 46.2 us (0.915)
  Pallas kernels: 47.3 us -> 44.3 us
  local copies, waits for them, and re-layouts: 2.95 us -> 1.67 us
    pallas_call x1, Pallas kernels: 47.3 us -> 44.3 us  [on_device(): pl.pallas_call(functools.partial(kernel, n_rows, n_heads), out_shape=jax....]
    reshape x1 -> x0, local copies, waits for them, and re-layouts: 1.28 us -> none  [on_device(): enc_gain.reshape(1, width)]
where the time goes in v2:
time: 46.2 us; the launch traced here: 46 us
  Pallas kernels  44.3 us (96%)
  local copies, waits for them, and re-layouts  1.67 us (4%)
    pallas_call x1, Pallas kernels, on_device(): pl.pallas_call(functools.partial(kernel, n_rows, n_heads), out_shape=jax....  44.3 us
    unnamed x1, local copies, waits for them, and re-layouts  1.67 us

profile of v2, /device:TPU:0, one launch (start us, length us, event | category | flops | bytes accessed | tf_op | source)
XLA Modules:
  0.0 46.0 jit_solution(15614971207597157559)
XLA Ops:
  0.0 44.3 %shard_map.73 = bf16[128,1024]{1,0:T(8,128)(2,1)} custom-call(s32[3]{0:T(128)} %length_ref.1, bf16[128,4096]{1,0:T(8,128)(2,1)} %queries_ref.1, bf16[48,1024]{1,0:T(8,128)(2,1)} %passages_ref.1, bf16[1024]{0:T(1024)(128)(2,1)} %gain_ref.1, bf16[1024,4096]{1,0:T(8,128)(2,1)} %key_ref.1, bf16[1024,4096]{1,0:T(8,128)(2,1)} %value_ref.1, bf16[4096,1024]{1,0:T(8,128)(2,1)} %outw_ref.1), custom_call_target="tpu_custom_call" | custom-call | tf_op jit(solution)/shard_map/pallas_call | solution.py:373
  44.3 1.7 %copy.9 = bf16[128,1024]{1,0:T(8,128)(2,1)} copy(bf16[128,1024]{1,0:T(8,128)(2,1)} %shard_map.73) | data formatting | bytes 524288

commit v3 on v2

--- a/solution.py
+++ b/solution.py
@@ -14,7 +14,7 @@
 MESH = pl.DeviceIdType.MESH
 LOADS = 4
 GROUP = 2 * DK
-OUT_CHUNK = 256
+OUT_CHUNK = 512
 
 
 def flip(index, bits):
@@ -68,7 +68,7 @@
     half = inner // 2
     n_pass = length_ref.shape[0]
     n_z = n_rows // 4
-    wide = width * 5 // 8
+    wide = width * 4 // 8
     narrow = width - wide
 
     me = lax.axis_index("rows")

time: 46.2 us -> 45.6 us (0.987)
  Pallas kernels: 44.3 us -> 43.7 us
    pallas_call x1, Pallas kernels: 44.3 us -> 43.7 us  [on_device(): pl.pallas_call(functools.partial(kernel, n_rows, n_heads), out_shape=jax....]
where the time goes in v3:
time: 45.6 us; the launch traced here: 45.4 us
  Pallas kernels  43.7 us (96%)
  local copies, waits for them, and re-layouts  1.67 us (4%)
    pallas_call x1, Pallas kernels, on_device(): pl.pallas_call(functools.partial(kernel, n_rows, n_heads), out_shape=jax....  43.7 us
    unnamed x1, local copies, waits for them, and re-layouts  1.67 us

profile of v3, /device:TPU:0, one launch (start us, length us, event | category | flops | bytes accessed | tf_op | source)
XLA Modules:
  0.0 45.4 jit_solution(17072077748049386612)
XLA Ops:
  0.0 43.7 %shard_map.73 = bf16[128,1024]{1,0:T(8,128)(2,1)} custom-call(s32[3]{0:T(128)} %length_ref.1, bf16[128,4096]{1,0:T(8,128)(2,1)} %queries_ref.1, bf16[48,1024]{1,0:T(8,128)(2,1)} %passages_ref.1, bf16[1024]{0:T(1024)(128)(2,1)} %gain_ref.1, bf16[1024,4096]{1,0:T(8,128)(2,1)} %key_ref.1, bf16[1024,4096]{1,0:T(8,128)(2,1)} %value_ref.1, bf16[4096,1024]{1,0:T(8,128)(2,1)} %outw_ref.1), custom_call_target="tpu_custom_call" | custom-call | tf_op jit(solution)/shard_map/pallas_call | solution.py:373
  43.7 1.7 %copy.9 = bf16[128,1024]{1,0:T(8,128)(2,1)} copy(bf16[128,1024]{1,0:T(8,128)(2,1)} %shard_map.73) | data formatting | bytes 524288
